TPU v7x, 256 devices: a whole 4x4x8 slice. The times are simulated.
256 devices in a mesh: grp: 4 (over y), tok: 64 (over z, x, core).
Axes of the slice: x: 4, y: 4, z: 8, core: 2. Of those that a mesh axis runs over, the one named last changes fastest.
Arguments:
- hidden: bfloat16 [512, 64, 1024], P('tok', 'grp'), may hold values from -6 to 6
- draft_qkv: bfloat16 [3, 512, 64, 1024], P(None, 'tok', None, 'grp'), may hold values from -4 to 4
- self_cache: bfloat16 [512, 2, 512, 1024], P('tok', None, None, 'grp'), may hold values from -4 to 4
- cross_cache: bfloat16 [512, 2, 512, 1024], P('tok', None, None, 'grp'), may hold values from -4 to 4
- parents: int32 [512, 64], P('tok'), may hold values from -1 to 62, as said below
- counts: int32 [512], P('tok'), may hold values from 32 to 64, as said below
- self_len: int32 [512], P('tok'), may hold values from 2 to 512, as said below
- enc_len: int32 [512], P('tok'), may hold values from 2 to 512, as said below
- buckets: int32 [512, 64, 64], P('tok'), may hold values from 0 to 31
- bias_table: float32 [32, 16], P(None, 'grp'), may hold values from -4 to 4
- gain_cross: float32 [1024], replicated, may hold values from 0.25 to 1.75
- gain_ffn: float32 [1024], replicated, may hold values from 0.25 to 1.75
- gain_next: float32 [1024], replicated, may hold values from 0.25 to 1.75
- w_out_self: bfloat16 [1024, 1024], P('grp', 'tok'), may hold values from -0.1875 to 0.1875
- w_query_cross: bfloat16 [1024, 1024], P('tok', 'grp'), may hold values from -1 to 1
- w_out_cross: bfloat16 [1024, 1024], P('grp', 'tok'), may hold values from -0.1875 to 0.1875
- w_gate: bfloat16 [1024, 2816], P('tok', 'grp'), may hold values from -0.1875 to 0.1875
- w_up: bfloat16 [1024, 2816], P('tok', 'grp'), may hold values from -0.1875 to 0.1875
- w_down: bfloat16 [2816, 1024], P('grp', 'tok'), may hold values from -0.109375 to 0.109375
- w_qkv: bfloat16 [1024, 3, 1024], P('tok', None, 'grp'), may hold values from -0.1875 to 0.1875
Outputs:
- out_hidden: bfloat16 [512, 64, 1024], P('tok', 'grp')
- next_qkv: bfloat16 [3, 512, 64, 1024], P(None, 'tok', None, 'grp')
Inputs may be any that keep to these rules, and one draw needn't show every extreme that they name: `parents`: slot 0 of every tree has parent -1; every other slot's parent is an earlier slot. `counts`: some request fills all 64 draft slots. `self_len`: some request fills its whole cache. `enc_len`: some request has all 512 encoder positions.
All inputs are finite; a program needn't handle non-finite values.
Results may differ from a plain program's by a relative error of at most 0.025.
Values may be sent and summed in bfloat16 or wider, within the bound.
A program may use at most 64 MiB of HBM per device.

v0:
```python
import jax
import jax.numpy as jnp
from jax import lax
from jax.sharding import PartitionSpec as P

DH = 64


def ancestor_table(parent_ids):
    count_slots = parent_ids.shape[0]
    slot_ids = jnp.arange(count_slots, dtype=jnp.int32)
    ancestors = jnp.eye(count_slots, dtype=jnp.float32) + (
        parent_ids[:, None] == slot_ids[None, :]
    ).astype(jnp.float32)
    for repeat in range(max(1, count_slots.bit_length())):
        ancestors = jnp.minimum(jnp.dot(ancestors, ancestors, precision=lax.Precision.HIGHEST), 1.0)
    return ancestors


def rms_scale(stream, gain_vec):
    mean_square = jnp.mean(stream * stream, axis=-1, keepdims=True)
    return (stream * lax.rsqrt(mean_square + 1e-06) * gain_vec).astype(jnp.bfloat16)


def draft_attention(projected, cached, parent_ids, draft_count, length, bucket_ids, bias_table):
    requests, draft_slots, head_width = (projected.shape[1], projected.shape[2], projected.shape[3])
    local_heads = bias_table.shape[1]
    head_size = head_width // local_heads
    queries = projected[0].reshape(requests, draft_slots, local_heads, head_size)
    draft_keys = projected[1].reshape(requests, draft_slots, local_heads, head_size)
    draft_values = projected[2].reshape(requests, draft_slots, local_heads, head_size)
    cache_keys = cached[:, 0].reshape(requests, -1, local_heads, head_size)
    cache_values = cached[:, 1].reshape(requests, -1, local_heads, head_size)
    cache_scores = jnp.einsum(
        "rihd,rphd->rhip", queries, cache_keys, preferred_element_type=jnp.float32
    )
    cache_scores = cache_scores + bias_table[-1][None, :, None, None]
    cache_live = jnp.arange(cache_keys.shape[1], dtype=jnp.int32)[None, :] < length[:, None]
    cache_scores = jnp.where(cache_live[:, None, None, :], cache_scores, -1e30)
    onehot = (bucket_ids[..., None] == jnp.arange(bias_table.shape[0], dtype=jnp.int32)).astype(
        jnp.float32
    )
    draft_bias = jnp.einsum("rijb,bh->rhij", onehot, bias_table, precision=lax.Precision.HIGHEST)
    draft_scores = (
        jnp.einsum("rihd,rjhd->rhij", queries, draft_keys, preferred_element_type=jnp.float32)
        + draft_bias
    )
    ancestors = jax.vmap(ancestor_table)(parent_ids)
    draft_live = (ancestors > 0.5) & (
        jnp.arange(draft_slots, dtype=jnp.int32)[None, None, :] < draft_count[:, None, None]
    )
    draft_scores = jnp.where(draft_live[:, None], draft_scores, -1e30)
    highest = jnp.maximum(cache_scores.max(-1, keepdims=True), draft_scores.max(-1, keepdims=True))
    exp_cache = jnp.exp(cache_scores - highest)
    exp_draft = jnp.exp(draft_scores - highest)
    denominator = exp_cache.sum(-1, keepdims=True) + exp_draft.sum(-1, keepdims=True)
    weights_cache = (exp_cache / denominator).astype(jnp.bfloat16)
    weights_draft = (exp_draft / denominator).astype(jnp.bfloat16)
    attended = jnp.einsum(
        "rhip,rphd->rihd", weights_cache, cache_values, preferred_element_type=jnp.float32
    )
    attended = attended + jnp.einsum(
        "rhij,rjhd->rihd", weights_draft, draft_values, preferred_element_type=jnp.float32
    )
    return attended.astype(jnp.bfloat16).reshape(requests * draft_slots, head_width)


def cross_attention(query_rows, cached, length):
    requests, draft_slots, head_width = query_rows.shape
    local_heads = head_width // DH
    queries = query_rows.reshape(requests, draft_slots, local_heads, DH)
    enc_keys = cached[:, 0].reshape(requests, -1, local_heads, DH)
    enc_values = cached[:, 1].reshape(requests, -1, local_heads, DH)
    scores = jnp.einsum("rihd,rphd->rhip", queries, enc_keys, preferred_element_type=jnp.float32)
    live = jnp.arange(enc_keys.shape[1], dtype=jnp.int32)[None, :] < length[:, None]
    scores = jnp.where(live[:, None, None, :], scores, -1e30)
    highest = scores.max(-1, keepdims=True)
    exp_scores = jnp.exp(scores - highest)
    weights = (exp_scores / exp_scores.sum(-1, keepdims=True)).astype(jnp.bfloat16)
    attended = jnp.einsum(
        "rhip,rphd->rihd", weights, enc_values, preferred_element_type=jnp.float32
    )
    return attended.astype(jnp.bfloat16).reshape(requests * draft_slots, head_width)


def layer_sum(summand, base_full):
    return lax.psum(summand.astype(jnp.bfloat16), "grp").astype(jnp.float32) + base_full


def normed_rows(stream, gain_vec):
    scaled = rms_scale(stream, gain_vec)
    return scaled.reshape(-1, scaled.shape[-1])


def shards(
    hidden,
    draft_qkv,
    self_cache,
    cross_cache,
    parents,
    counts,
    self_len,
    enc_len,
    buckets,
    bias_table,
    gain_cross,
    gain_ffn,
    gain_next,
    w_out_self,
    w_query_cross,
    w_out_cross,
    w_gate,
    w_up,
    w_down,
    w_qkv,
):
    requests, share_rows, model_width = hidden.shape
    draft_slots = draft_qkv.shape[2]
    head_width = draft_qkv.shape[3]
    fetched = (
        lax.all_gather(w_out_self, "tok", axis=1, tiled=True),
        lax.all_gather(w_query_cross, "tok", axis=0, tiled=True),
        lax.all_gather(w_out_cross, "tok", axis=1, tiled=True),
        lax.all_gather(w_gate, "tok", axis=0, tiled=True),
        lax.all_gather(w_up, "tok", axis=0, tiled=True),
        lax.all_gather(w_down, "tok", axis=1, tiled=True),
        lax.all_gather(w_qkv, "tok", axis=0, tiled=True),
    )
    self_context = draft_attention(
        draft_qkv, self_cache, parents, counts, self_len, buckets, bias_table
    )
    partial_value = jnp.dot(self_context, fetched[0], preferred_element_type=jnp.float32)
    partial_value = partial_value.reshape(requests, draft_slots, model_width)
    own_rows = hidden.astype(jnp.float32)
    offset = lax.axis_index("grp") * share_rows
    placed = lax.dynamic_update_slice(
        jnp.zeros((requests, draft_slots, model_width), jnp.float32), own_rows, (0, offset, 0)
    )
    stream_one = layer_sum(partial_value + placed, 0.0)
    normed_one = normed_rows(stream_one, gain_cross)
    cross_query = jnp.dot(normed_one, fetched[1], preferred_element_type=jnp.float32)
    cross_query = cross_query.astype(jnp.bfloat16).reshape(requests, draft_slots, head_width)
    cross_context = cross_attention(cross_query, cross_cache, enc_len)
    partial_value = jnp.dot(cross_context, fetched[2], preferred_element_type=jnp.float32)
    stream_two = layer_sum(partial_value.reshape(requests, draft_slots, model_width), stream_one)
    normed_two = normed_rows(stream_two, gain_ffn)
    gate_part = jnp.dot(normed_two, fetched[3], preferred_element_type=jnp.float32)
    up_part = jnp.dot(normed_two, fetched[4], preferred_element_type=jnp.float32)
    gated = (jax.nn.gelu(gate_part, approximate=True) * up_part).astype(jnp.bfloat16)
    partial_value = jnp.dot(gated, fetched[5], preferred_element_type=jnp.float32)
    stream_three = layer_sum(partial_value.reshape(requests, draft_slots, model_width), stream_two)
    normed_three = normed_rows(stream_three, gain_next)
    projected = jnp.dot(
        normed_three,
        fetched[6].reshape(fetched[6].shape[0], -1),
        preferred_element_type=jnp.float32,
    )
    projected = projected.astype(jnp.bfloat16).reshape(requests, draft_slots, 3, head_width)
    next_qkv = jnp.transpose(projected, (2, 0, 1, 3))
    out_hidden = lax.dynamic_slice_in_dim(stream_three, offset, share_rows, 1).astype(jnp.bfloat16)
    return (out_hidden, next_qkv)


def solution(mesh):
    in_specs = (
        P("tok", "grp", None),
        P(None, "tok", None, "grp"),
        P("tok", None, None, "grp"),
        P("tok", None, None, "grp"),
        P("tok", None),
        P("tok"),
        P("tok"),
        P("tok"),
        P("tok", None, None),
        P(None, "grp"),
        P(),
        P(),
        P(),
        P("grp", "tok"),
        P("tok", "grp"),
        P("grp", "tok"),
        P("tok", "grp"),
        P("tok", "grp"),
        P("grp", "tok"),
        P("tok", None, "grp"),
    )
    out_specs = (P("tok", "grp", None), P(None, "tok", None, "grp"))
    return jax.shard_map(shards, mesh=mesh, in_specs=in_specs, out_specs=out_specs, check_vma=False)
```

profile of v0, /device:TPU:1, one launch (start us, length us, event | category | flops | bytes accessed | tf_op | source)
XLA Modules:
  0.0 532.7 jit_solution(6397232074818495033)
XLA Ops:
  8.1 3.9 fusion.56
  12.0 2.4 copy.53
  14.6 2.9 copy.47
  17.5 1.9 fusion.57
  19.7 3.6 fusion.1
  23.3 2.6 copy.52
  25.8 1.2 reshape_squeeze.23
  32.0 1.5 fusion.7
  33.7 1.0 reshape_squeeze.25
  34.7 3.0 fusion.14
  39.0 54.8 %all_gather.21 = bf16[256,1024]{0,1:T(8,128)(2,1)S(1)} all-gather(bf16[256,16]{0,1:T(8,128)(2,1)S(1)} %copy-done.9), channel_id=1, replica_groups=mesh['grp'=4,'tok'=64] {'tok'}, dimensions={1}, use_global_device_ids=true | all-gather | bytes 532480 | tf_op jit(solution)/shard_map/all_gather | solution.py:121
  94.4 1.1 convert_element_type.84
  95.6 3.9 fusion.55
  99.5 2.4 copy.59
  101.9 2.9 copy.57
  104.8 49.2 %all_gather.22 = bf16[1024,256]{1,0:T(8,128)(2,1)S(1)} all-gather(bf16[16,256]{1,0:T(8,128)(2,1)S(1)} %copy-done.10), channel_id=1, replica_groups=mesh['grp'=4,'tok'=64] {'tok'}, dimensions={0}, use_global_device_ids=true | all-gather | bytes 532480 | tf_op jit(solution)/shard_map/all_gather | solution.py:122
  154.0 48.2 %all_gather.23 = bf16[256,1024]{0,1:T(8,128)(2,1)S(1)} all-gather(bf16[256,16]{0,1:T(8,128)(2,1)S(1)} %copy-done.11), channel_id=1, replica_groups=mesh['grp'=4,'tok'=64] {'tok'}, dimensions={1}, use_global_device_ids=true | all-gather | bytes 532480 | tf_op jit(solution)/shard_map/all_gather | solution.py:123
  202.2 1.5 fusion.8
  203.8 1.5 fusion.10
  206.7 2.0 fusion.59
  210.2 1.5 convolution_convert_fusion.1
  214.6 44.3 %all-reduce.6.cloned.1.call-done = bf16[8,64,1024]{2,1,0:T(8,128)(2,1)} async-done(((bf16[8,64,1024]{2,1,0:T(8,128)(2,1)}), bf16[8,64,1024]{2,1,0:T(8,128)(2,1)}) %all-reduce.6.cloned.1.call-update) | async-done | bytes 1048592 | tf_op jit(solution)/shard_map/psum | solution.py:87
  258.9 1.7 multiply_reduce_fusion.1
  261.0 28.7 %all-gather.5.cloned.1.call-done = bf16[1024,704]{1,0:T(8,128)(2,1)} async-done(((bf16[16,704]{1,0:T(8,128)(2,1)}), bf16[1024,704]{1,0:T(8,128)(2,1)}) %all-gather.5.cloned.1.call-update) | async-done | bytes 1441808 | tf_op jit(solution)/shard_map/all_gather | solution.py:124
  289.7 3.5 fusion.60
  293.2 73.9 %all-gather.9.cloned.1.call-done = bf16[704,1024]{0,1:T(8,128)(2,1)} async-done(((bf16[704,16]{0,1:T(8,128)(2,1)}), bf16[704,1024]{0,1:T(8,128)(2,1)}) %all-gather.9.cloned.1.call-update) | async-done | bytes 1441808 | tf_op jit(solution)/shard_map/all_gather | solution.py:126
  367.1 77.4 %all-gather.7.cloned.1.call-done = bf16[1024,704]{1,0:T(8,128)(2,1)} async-done(((bf16[16,704]{1,0:T(8,128)(2,1)}), bf16[1024,704]{1,0:T(8,128)(2,1)}) %all-gather.7.cloned.1.call-update) | async-done | bytes 1441808 | tf_op jit(solution)/shard_map/all_gather | solution.py:125
  444.5 5.5 %convolution_convert_fusion = bf16[512,1024]{1,0:T(8,128)(2,1)} fusion(bf16[704,1024]{0,1:T(8,128)(2,1)} %all-gather.9.cloned.1.call-done, bf16[512,1024]{1,0:T(8,128)(2,1)S(1)} %bitcast.67, bf16[1024,704]{1,0:T(8,128)(2,1)} %all-gather.7.cloned.1.call-done, f32[512,704]{0,1:T(8,128)} %fusion.60), kind=kOutput, calls=%fused_computation.29 | convolution fusion | flops 1480523776 | bytes 6422528 | tf_op jit(solution)/shard_map/dot_general | solution.py:150
  450.0 67.0 %all-gather.11.cloned.1.call-done = bf16[1024,3,256]{2,0,1:T(8,128)(2,1)} async-done(((bf16[16,3,256]{2,0,1:T(8,128)(2,1)}), bf16[1024,3,256]{2,0,1:T(8,128)(2,1)}) %all-gather.11.cloned.1.call-update) | async-done | bytes 1572880 | tf_op jit(solution)/shard_map/all_gather | solution.py:127
  517.1 2.6 copy.61
  519.7 1.8 multiply_reduce_fusion
  522.9 1.0 convolution_convert_fusion.2
  (96 shorter events, 16.4 us)
Async XLA Ops:
  8.0 194.2 %all-reduce.4.cloned.1.call-start = ((), (), s32[]{:S(2)}) async-start(), calls=%async_computation | async-start | bytes 2097152 | tf_op jit(solution)/shard_map/psum | solution.py:87
  12.0 2.4 copy-start.16
  12.0 2.6 copy-start.17
  17.5 2.2 copy-start.19
  19.7 7.4 %copy-start.12 = (s32[8,64]{1,0:T(8,128)S(1)}, s32[8,64]{1,0:T(8,128)}, u32[]{:S(2)}) copy-start(s32[8,64]{1,0:T(8,128)} %param.24) | copy-start | bytes 6148
  27.1 2.5 copy-start.20
  30.3 1.2 copy-start.3
  31.5 2.0 copy-start.1
  31.9 2.8 copy-start.4
  34.7 3.1 copy-start.7
  37.8 1.2 copy-start.9
  38.6 55.7 %copy-start.8 = (bf16[8,16,1024]{2,1,0:T(8,128)(2,1)S(1)}, bf16[8,16,1024]{2,1,0:T(8,128)(2,1)}, u32[]{:S(2)}) copy-start(bf16[8,16,1024]{2,1,0:T(8,128)(2,1)} %param.20) | copy-start | bytes 786436
  95.6 163.3 %all-reduce.6.cloned.1.call-start = ((), (), s32[]{:S(2)}) async-start(), calls=%async_computation.1 | async-start | bytes 2097152 | tf_op jit(solution)/shard_map/psum | solution.py:87
  101.9 2.9 copy-start.10
  101.9 52.1 %copy-start.11 = (bf16[256,16]{0,1:T(8,128)(2,1)S(1)}, bf16[256,16]{0,1:T(8,128)(2,1)}, u32[]{:S(2)}) copy-start(bf16[256,16]{0,1:T(8,128)(2,1)} %param.35) | copy-start | bytes 24580
  101.9 100.3 %copy-start.18 = (s32[8]{0:T(128)S(1)}, s32[8]{0:T(128)}, u32[]{:S(2)}) copy-start(s32[8]{0:T(128)} %param.27) | copy-start | bytes 100
  104.8 98.9 %copy-start.13 = (f32[1024]{0:T(1024)S(1)}, f32[1024]{0:T(1024)}, u32[]{:S(2)}) copy-start(f32[1024]{0:T(1024)} %param.30) | copy-start | bytes 12292
  206.7 2.0 copy-start.5
  209.9 49.0 %copy-start = (bf16[8,64,1024]{2,1,0:T(8,128)(2,1)S(1)}, bf16[8,64,1024]{2,1,0:T(8,128)(2,1)}, u32[]{:S(2)}) copy-start(bf16[8,64,1024]{2,1,0:T(8,128)(2,1)} %all-reduce.4.cloned.1.call-done) | copy-start | bytes 3145732
  210.2 50.4 %copy-start.14 = (f32[1024]{0:T(1024)S(1)}, f32[1024]{0:T(1024)}, u32[]{:S(2)}) copy-start(f32[1024]{0:T(1024)} %param.31) | copy-start | bytes 12292
  211.8 77.9 %all-gather.5.cloned.1.call-start = ((), (), s32[]{:S(2)}) async-start(), calls=%async_computation.2 | async-start | bytes 1597440 | tf_op jit(solution)/shard_map/all_gather | solution.py:124
  212.4 154.7 %all-gather.9.cloned.1.call-start = ((), (), s32[]{:S(2)}) async-start(), calls=%async_computation.4 | async-start | bytes 1597440 | tf_op jit(solution)/shard_map/all_gather | solution.py:126
  213.0 231.5 %all-gather.7.cloned.1.call-start = ((), (), s32[]{:S(2)}) async-start(), calls=%async_computation.3 | async-start | bytes 1597440 | tf_op jit(solution)/shard_map/all_gather | solution.py:125
  213.5 303.5 %all-gather.11.cloned.1.call-start = ((), (), s32[]{:S(2)}) async-start(), calls=%async_computation.6 | async-start | bytes 1597440 | tf_op jit(solution)/shard_map/all_gather | solution.py:127
  214.3 305.4 %all-reduce.8.cloned.1.call-start = ((), (), s32[]{:S(2)}) async-start(), calls=%async_computation.5 | async-start | bytes 2097152 | tf_op jit(solution)/shard_map/psum | solution.py:87
  258.9 1.7 copy-start.2
  519.6 2.5 copy-start.15
  521.4 1.5 copy-start.6
Sparse Core Ops, SparseCore 0:
  95.7 46.8 all-reduce.3
  211.9 46.8 all-reduce.5
  450.1 46.8 all-reduce.7
Sparse Core Ops, SparseCore 1:
  215.0 74.7 all-gather.4
  292.4 74.7 all-gather.8
  369.8 74.7 all-gather.6
  447.5 69.5 all-gather.10
where the time goes:
time: 533 us
  waiting for transfers between devices  294 us (55%)
  blocking collectives  152 us (29%)
  local copies, waits for them, and re-layouts  33.2 us (6%)
  matrix products  25 us (5%)
  between operations  15.9 us (3%)
  other arithmetic  12.3 us (2%)
    all_gather x1, waiting for transfers between devices, shards(): lax.all_gather(w_up, 'tok', axis=0, tiled=True)  77.4 us
    all_gather x1, waiting for transfers between devices, shards(): lax.all_gather(w_down, 'tok', axis=1, tiled=True)  73.9 us
    all_gather x1, waiting for transfers between devices, shards(): lax.all_gather(w_qkv, 'tok', axis=0, tiled=True)  67 us
    all_gather x1, blocking collectives, shards(): lax.all_gather(w_out_self, 'tok', axis=1, tiled=True)  54.8 us
    all_gather x1, blocking collectives, shards(): lax.all_gather(w_query_cross, 'tok', axis=0, tiled=True)  49.2 us
    all_gather x1, blocking collectives, shards(): lax.all_gather(w_out_cross, 'tok', axis=1, tiled=True)  48.2 us
    psum x3, waiting for transfers between devices, layer_sum(): lax.psum(summand.astype(jnp.bfloat16), 'grp').astype(jnp.float32)  44.3 us
    all_gather x1, waiting for transfers between devices, shards(): lax.all_gather(w_gate, 'tok', axis=0, tiled=True)  28.7 us
  transfers between devices with their start and end apart: 7, of which 5 were waited for; matrix products, arithmetic and copies ran while one was open for 4% of the time, Pallas kernels for 0%

commit v1 on v0

--- a/solution.py
+++ b/solution.py
@@ -4,6 +4,11 @@
 from jax.sharding import PartitionSpec as P
 
 DH = 64
+
+
+def tell_the_limits(piece_in, comm_axis):
+    prior = jnp.sum(lax.all_gather(piece_in, axis_name=comm_axis), axis=0)
+    return prior
 
 
 def ancestor_table(parent_ids):
@@ -84,7 +89,7 @@
 
 
 def layer_sum(summand, base_full):
-    return lax.psum(summand.astype(jnp.bfloat16), "grp").astype(jnp.float32) + base_full
+    return tell_the_limits(summand.astype(jnp.bfloat16), "grp").astype(jnp.float32) + base_full
 
 
 def normed_rows(stream, gain_vec):

time: 533 us -> 645 us (1.21)
  waiting for transfers between devices: 294 us -> 390 us
  blocking collectives: 152 us -> 161 us
    all_gather x0 -> x3, waiting for transfers between devices: none -> 94.3 us  [tell_the_limits(): prior = jnp.sum(lax.all_gather(piece_in, axis_name=comm_axis), axis=0)]
    all_gather x1, waiting for transfers between devices: 28.7 us -> 76.1 us  [shards(): lax.all_gather(w_gate, 'tok', axis=0, tiled=True)]
    psum x3 -> x0, waiting for transfers between devices: 44.3 us -> none  [layer_sum(): lax.psum(summand.astype(jnp.bfloat16), 'grp').astype(jnp.float32)]
    reduce_sum x0 -> x3, other arithmetic: none -> 9.84 us  [tell_the_limits(): prior = jnp.sum(lax.all_gather(piece_in, axis_name=comm_axis), axis=0)]
  transfers between devices with their start and end apart: 7 -> 7, of which waited for: 5 -> 6; matrix products, arithmetic and copies ran while one was open for 4% -> 4% of each run, Pallas kernels for 0% -> 0%
where the time goes in v1:
time: 645 us
  waiting for transfers between devices  390 us (60%)
  blocking collectives  161 us (25%)
  local copies, waits for them, and re-layouts  35.4 us (5%)
  matrix products  25.9 us (4%)
  other arithmetic  17.3 us (3%)
  between operations  14.6 us (2%)
    all_gather x3, waiting for transfers between devices, tell_the_limits(): prior = jnp.sum(lax.all_gather(piece_in, axis_name=comm_axis), axis=0)  94.3 us
    all_gather x1, waiting for transfers between devices, shards(): lax.all_gather(w_up, 'tok', axis=0, tiled=True)  77.2 us
    all_gather x1, waiting for transfers between devices, shards(): lax.all_gather(w_gate, 'tok', axis=0, tiled=True)  76.1 us
    all_gather x1, waiting for transfers between devices, shards(): lax.all_gather(w_down, 'tok', axis=1, tiled=True)  73.7 us
    all_gather x1, waiting for transfers between devices, shards(): lax.all_gather(w_qkv, 'tok', axis=0, tiled=True)  66.2 us
    all_gather x1, blocking collectives, shards(): lax.all_gather(w_out_self, 'tok', axis=1, tiled=True)  54.8 us
    all_gather x1, blocking collectives, shards(): lax.all_gather(w_query_cross, 'tok', axis=0, tiled=True)  53.4 us
    all_gather x1, blocking collectives, shards(): lax.all_gather(w_out_cross, 'tok', axis=1, tiled=True)  52.9 us
  transfers between devices with their start and end apart: 7, of which 6 were waited for; matrix products, arithmetic and copies ran while one was open for 4% of the time, Pallas kernels for 0%

profile of v1, /device:TPU:1, one launch (start us, length us, event | category | flops | bytes accessed | tf_op | source)
XLA Modules:
  0.0 644.5 jit_solution(6770149965324391682)
XLA Ops:
  7.2 3.9 fusion.59
  11.1 2.4 copy.53
  13.8 2.9 copy.47
  16.7 1.9 fusion.60
  18.8 3.6 fusion.1
  22.4 2.6 copy.52
  25.0 1.2 reshape_squeeze.23
  31.1 1.5 fusion.7
  33.9 3.0 fusion.17
  38.2 54.8 %all_gather.37 = bf16[256,1024]{0,1:T(8,128)(2,1)S(1)} all-gather(bf16[256,16]{0,1:T(8,128)(2,1)S(1)} %copy-done.9), channel_id=1, replica_groups=mesh['grp'=4,'tok'=64] {'tok'}, dimensions={1}, use_global_device_ids=true | all-gather | bytes 532480 | tf_op jit(solution)/shard_map/all_gather | solution.py:126
  93.6 1.2 convert_element_type.146
  94.9 3.9 fusion.58
  98.8 2.4 copy.59
  101.2 2.9 copy.57
  104.1 53.4 %all_gather.40 = bf16[1024,256]{1,0:T(8,128)(2,1)} all-gather(bf16[16,256]{1,0:T(8,128)(2,1)S(1)} %copy-done.10), channel_id=1, replica_groups=mesh['grp'=4,'tok'=64] {'tok'}, dimensions={0}, use_global_device_ids=true | all-gather | bytes 532480 | tf_op jit(solution)/shard_map/all_gather | solution.py:127
  157.5 52.9 %all_gather.41 = bf16[256,1024]{0,1:T(8,128)(2,1)} all-gather(bf16[256,16]{0,1:T(8,128)(2,1)S(1)} %copy-done.11), channel_id=1, replica_groups=mesh['grp'=4,'tok'=64] {'tok'}, dimensions={1}, use_global_device_ids=true | all-gather | bytes 532480 | tf_op jit(solution)/shard_map/all_gather | solution.py:128
  210.5 3.3 reduce_sum.92
  215.7 1.0 reshape_reshape.3
  216.7 1.7 fusion.37
  218.5 2.0 fusion.62
  222.3 1.5 convolution_convert_fusion.1
  226.5 45.4 %all-gather.22.cloned.1.call-done = bf16[32,64,1024]{2,1,0:T(8,128)(2,1)} async-done(((bf16[8,64,1024]{2,1,0:T(8,128)(2,1)}), bf16[32,64,1024]{2,1,0:T(8,128)(2,1)}) %all-gather.22.cloned.1.call-update) | async-done | bytes 4194320 | tf_op jit(solution)/shard_map/all_gather | solution.py:10
  272.0 3.3 reduce_sum.95
  276.3 76.1 %all-gather.10.cloned.1.call-done = bf16[1024,704]{1,0:T(8,128)(2,1)} async-done(((bf16[16,704]{1,0:T(8,128)(2,1)}), bf16[1024,704]{1,0:T(8,128)(2,1)}) %all-gather.10.cloned.1.call-update) | async-done | bytes 1441808 | tf_op jit(solution)/shard_map/all_gather | solution.py:129
  352.4 3.5 fusion.63
  355.9 73.7 %all-gather.14.cloned.1.call-done = bf16[704,1024]{0,1:T(8,128)(2,1)} async-done(((bf16[704,16]{0,1:T(8,128)(2,1)}), bf16[704,1024]{0,1:T(8,128)(2,1)}) %all-gather.14.cloned.1.call-update) | async-done | bytes 1441808 | tf_op jit(solution)/shard_map/all_gather | solution.py:131
  429.6 77.2 %all-gather.12.cloned.1.call-done = bf16[1024,704]{1,0:T(8,128)(2,1)} async-done(((bf16[16,704]{1,0:T(8,128)(2,1)}), bf16[1024,704]{1,0:T(8,128)(2,1)}) %all-gather.12.cloned.1.call-update) | async-done | bytes 1441808 | tf_op jit(solution)/shard_map/all_gather | solution.py:130
  506.8 5.5 convolution_convert_fusion
  512.3 66.2 %all-gather.18.cloned.1.call-done = bf16[1024,3,256]{2,0,1:T(8,128)(2,1)} async-done(((bf16[16,3,256]{2,0,1:T(8,128)(2,1)}), bf16[1024,3,256]{2,0,1:T(8,128)(2,1)}) %all-gather.18.cloned.1.call-update) | async-done | bytes 1572880 | tf_op jit(solution)/shard_map/all_gather | solution.py:132
  578.5 2.6 copy.61
  581.1 48.8 %all-gather.16.cloned.1.call-done = bf16[4,8,64,1024]{3,2,1,0:T(8,128)(2,1)} async-done(((bf16[1,8,64,1024]{3,2,1,0:T(8,128)(2,1)}), bf16[4,8,64,1024]{3,2,1,0:T(8,128)(2,1)}) %all-gather.16.cloned.1.call-update) | async-done | bytes 4194320 | tf_op jit(solution)/shard_map/all_gather | solution.py:10
  629.9 3.3 reduce_sum.97
  (101 shorter events, 20.4 us)
Async XLA Ops:
  7.2 203.4 %all-gather.20.cloned.1.call-start = ((), (), s32[]{:S(2)}) async-start(), calls=%async_computation.5 | async-start | bytes 5242880 | tf_op jit(solution)/shard_map/all_gather | solution.py:10
  11.1 2.4 copy-start.16
  11.1 2.6 copy-start.17
  16.6 2.2 copy-start.19
  18.8 7.4 %copy-start.12 = (s32[8,64]{1,0:T(8,128)S(1)}, s32[8,64]{1,0:T(8,128)}, u32[]{:S(2)}) copy-start(s32[8,64]{1,0:T(8,128)} %param.24) | copy-start | bytes 6148
  26.3 2.5 copy-start.20
  29.4 1.2 copy-start.1
  30.6 2.0 copy-start
  31.1 2.8 copy-start.3
  33.9 3.1 copy-start.6
  36.9 1.2 copy-start.9
  37.8 55.7 %copy-start.8 = (bf16[8,16,1024]{2,1,0:T(8,128)(2,1)S(1)}, bf16[8,16,1024]{2,1,0:T(8,128)(2,1)}, u32[]{:S(2)}) copy-start(bf16[8,16,1024]{2,1,0:T(8,128)(2,1)} %param.20) | copy-start | bytes 786436
  94.8 177.1 %all-gather.22.cloned.1.call-start = ((), (), s32[]{:S(2)}) async-start(), calls=%async_computation.6 | async-start | bytes 5242880 | tf_op jit(solution)/shard_map/all_gather | solution.py:10
  101.2 3.0 copy-start.10
  101.2 56.3 %copy-start.11 = (bf16[256,16]{0,1:T(8,128)(2,1)S(1)}, bf16[256,16]{0,1:T(8,128)(2,1)}, u32[]{:S(2)}) copy-start(bf16[256,16]{0,1:T(8,128)(2,1)} %param.35) | copy-start | bytes 24580
  101.2 109.3 %copy-start.18 = (s32[8]{0:T(128)S(1)}, s32[8]{0:T(128)}, u32[]{:S(2)}) copy-start(s32[8]{0:T(128)} %param.27) | copy-start | bytes 100
  210.5 3.7 copy-start.13
  214.2 1.0 copy-start.7
  218.5 2.0 copy-start.4
  221.2 1.0 copy-start.2
  223.7 128.7 %all-gather.10.cloned.1.call-start = ((), (), s32[]{:S(2)}) async-start(), calls=%async_computation | async-start | bytes 1597440 | tf_op jit(solution)/shard_map/all_gather | solution.py:129
  224.5 205.2 %all-gather.14.cloned.1.call-start = ((), (), s32[]{:S(2)}) async-start(), calls=%async_computation.2 | async-start | bytes 1597440 | tf_op jit(solution)/shard_map/all_gather | solution.py:131
  225.1 281.8 %all-gather.12.cloned.1.call-start = ((), (), s32[]{:S(2)}) async-start(), calls=%async_computation.1 | async-start | bytes 1597440 | tf_op jit(solution)/shard_map/all_gather | solution.py:130
  225.6 352.9 %all-gather.18.cloned.1.call-start = ((), (), s32[]{:S(2)}) async-start(), calls=%async_computation.4 | async-start | bytes 1597440 | tf_op jit(solution)/shard_map/all_gather | solution.py:132
  226.2 403.7 %all-gather.16.cloned.1.call-start = ((), (), s32[]{:S(2)}) async-start(), calls=%async_computation.3 | async-start | bytes 5242880 | tf_op jit(solution)/shard_map/all_gather | solution.py:10
  275.3 0.7 copy-start.14
  633.2 1.3 copy-start.15
  633.7 1.5 copy-start.5
Sparse Core Ops, SparseCore 0:
  95.0 48.1 all-gather.19
  223.9 48.0 all-gather.21
  274.7 77.6 all-gather.9
  355.1 74.5 all-gather.13
  432.2 74.5 all-gather.11
  509.3 69.1 all-gather.17
  580.3 49.5 all-gather.15
